TPU v7x, 128 devices: a whole 4x4x4 slice. The times are simulated.
128 devices in a mesh: rows: 16 (over z_lo, x, core), batch: 8 (over z_hi, y).
Axes of the slice: x: 4, y: 4, z: 4 (z_hi: 2, z_lo: 2; z = z_hi * 2 + z_lo), core: 2. Of those that a mesh axis runs over, the one named last changes fastest.
Arguments:
- bases: bfloat16 [49152, 2048], P('rows', 'batch'), may hold values from -30 to 30
- start: float32 [2048, 512], P('batch'), may hold values from -6 to 6
Outputs:
- modes: bfloat16 [49152, 512], P(('rows', 'batch'))
All inputs are finite; a program needn't handle non-finite values.
Results may differ from a plain program's by a relative error of at most 0.0041.
Values may be sent and summed in bfloat16 or wider, within the bound.
A program may use at most 128 MiB of HBM per device.

v0:
```python
import jax
import jax.numpy as jnp
from jax import lax
from jax.sharding import PartitionSpec as P

ITERS = 2


def inner_cols(left, right):
    return lax.dot_general(
        left, right, (((0,), (0,)), ((), ())), preferred_element_type=jnp.float32
    )


def on_device(bases, start):
    basis_width = bases.shape[1]
    group_count = lax.axis_size("batch")
    all_columns = basis_width * group_count
    energy = lax.psum(jnp.sum(jnp.square(bases.astype(jnp.float32))), ("rows", "batch"))
    diag_mean = energy / all_columns
    partial_value = inner_cols(bases, lax.all_gather(bases, "batch", axis=1, tiled=True))
    gram_rows = lax.psum(partial_value, "rows")
    q_own = start
    for iteration in range(ITERS):
        q_full = lax.all_gather(q_own, "batch", axis=0, tiled=True)
        lifted = jnp.dot(gram_rows, q_full, precision=lax.Precision.HIGHEST) / diag_mean + q_own
        local_correlation = lax.dot_general(
            lifted, lifted, (((0,), (0,)), ((), ())), precision=lax.Precision.HIGHEST
        )
        correlation = lax.psum(local_correlation, "batch")
        factor = jnp.linalg.cholesky(correlation)
        q_own = jax.scipy.linalg.solve_triangular(factor, lifted.T, lower=True).T
    q_low = q_own.astype(jnp.bfloat16)
    modes = lax.psum_scatter(
        jnp.dot(bases, q_low, preferred_element_type=jnp.float32),
        "batch",
        scatter_dimension=0,
        tiled=True,
    )
    return modes.astype(jnp.bfloat16)


def solution(mesh):
    in_specs = (P("rows", "batch"), P("batch", None))
    out_specs = P(("rows", "batch"), None)
    return jax.shard_map(
        on_device, mesh=mesh, in_specs=in_specs, out_specs=out_specs, check_vma=False
    )
```

profile of v0, /device:TPU:0, one launch (start us, length us, event | category | flops | bytes accessed | tf_op | source)
XLA Modules:
  0.0 1044.4 jit_solution(2930456255555356268)
XLA Ops:
  8.1 166.4 %all-gather.4.cloned.1.call-done = bf16[3072,2048]{1,0:T(8,128)(2,1)} async-done(((bf16[3072,256]{1,0:T(8,128)(2,1)}), bf16[3072,2048]{1,0:T(8,128)(2,1)}) %all-gather.4.cloned.1.call-update) | async-done | bytes 12582928 | tf_op jit(solution)/shard_map/all_gather | solution.py:21
  174.4 7.8 fusion.76
  182.3 1.4 multiply_reduce_fusion
  183.7 78.1 %psum.29 = f32[]{:T(128)} all-reduce(f32[]{:T(128)} %multiply_reduce_fusion), channel_id=1, replica_groups=mesh['rows'=16,'batch'=8] {'rows','batch'}, use_global_device_ids=true, to_apply=%region_2.0 | all-reduce | flops 1 | bytes 8 | tf_op jit(solution)/shard_map/psum | solution.py:19
  262.5 108.6 %all-reduce.5.cloned.1.call-done = f32[256,2048]{1,0:T(8,128)} async-done(((f32[256,2048]{1,0:T(8,128)}), f32[256,2048]{1,0:T(8,128)}) %all-reduce.5.cloned.1.call-update) | async-done | bytes 2097168 | tf_op jit(solution)/shard_map/psum | solution.py:22
  371.1 6.2 fusion
  377.3 2.1 fusion.77
  379.9 88.5 %all-reduce.7.cloned.1.call-done = f32[512,512]{0,1:T(8,128)} async-done(((f32[512,512]{0,1:T(8,128)}), f32[512,512]{0,1:T(8,128)}) %all-reduce.7.cloned.1.call-update) | async-done | bytes 1048592 | tf_op jit(solution)/shard_map/psum | solution.py:30
  468.5 2.7 copy.4
  471.2 1.4 fusion.2
  473.6 11.7 %cholesky.286 = f32[128,128]{1,0:T(8,128)S(1)} custom-call(f32[128,128]{1,0:T(8,128)S(1)} %cholesky.426), custom_call_target="Cholesky" | custom-call | tf_op jit(solution)/shard_map/jit(cholesky)/cholesky | solution.py:31
  485.4 9.8 custom-call.27
  497.8 11.7 %cholesky.305 = f32[128,128]{1,0:T(8,128)S(1)} custom-call(f32[128,128]{1,0:T(8,128)S(1)} %cholesky.430), custom_call_target="Cholesky" | custom-call | tf_op jit(solution)/shard_map/jit(cholesky)/cholesky | solution.py:31
  509.6 10.0 custom-call.28
  521.1 11.7 %cholesky.326 = f32[128,128]{1,0:T(8,128)S(1)} custom-call(f32[128,128]{1,0:T(8,128)S(1)} %cholesky.435), custom_call_target="Cholesky" | custom-call | tf_op jit(solution)/shard_map/jit(cholesky)/cholesky | solution.py:31
  533.6 9.8 custom-call.29
  544.8 11.7 %cholesky.343 = f32[128,128]{1,0:T(8,128)S(1)} custom-call(f32[128,128]{1,0:T(8,128)S(1)} %convolution_subtract_fusion.11), custom_call_target="Cholesky" | custom-call | tf_op jit(solution)/shard_map/jit(cholesky)/cholesky | solution.py:31
  561.8 11.7 %while.4 = (s32[]{:T(128)}, f32[512,512]{1,0:T(8,128)}, s32[4,2]{0,1:T(2,128)S(1)}, f32[4,128,128]{2,1,0:T(8,128)S(1)}, s32[]{:T(128)}) while((s32[]{:T(128)}, f32[512,512]{1,0:T(8,128)}, s32[4,2]{0,1:T(2,128)S(1)}, f32[4,128,128]{2,1,0:T(8,128)S(1)}, s32[]{:T(128)}) %tuple.52), condition=%wide.while_cond, body=%wide.while_body.sunk | while | flops 2 | bytes 131181 | solution.py:32
  562.5 2.3 bitcast_dynamic-update-slice_fusion.4
  565.4 2.3 bitcast_dynamic-update-slice_fusion.4
  568.4 2.3 bitcast_dynamic-update-slice_fusion.4
  571.3 2.2 bitcast_dynamic-update-slice_fusion.4
  573.5 39.3 %custom-call.30 = f32[4,128,128]{1,2,0:T(8,128)S(1)} custom-call(f32[4,128,128]{2,1,0:T(8,128)S(1)} %get-tuple-element.21), custom_call_target="InvertDiagBlocksLowerTriangular" | custom-call | tf_op jit(solution)/shard_map/jit(_solve_triangular)/triangular_solve | solution.py:32
  614.7 1.5 convolution_subtract_fusion.6
  616.5 1.7 convolution_subtract_fusion.5
  619.7 69.7 %all-gather.8.cloned.1.call-done = f32[2048,512]{1,0:T(8,128)} async-done(((f32[256,512]{1,0:T(8,128)}), f32[2048,512]{1,0:T(8,128)}) %all-gather.8.cloned.1.call-update) | async-done | bytes 4194320 | tf_op jit(solution)/shard_map/all_gather | solution.py:25
  689.4 6.3 bitcast_add_fusion.2
  695.7 2.1 fusion.3
  698.3 85.3 %all-reduce.9.cloned.1.call-done = f32[512,512]{0,1:T(8,128)} async-done(((f32[512,512]{0,1:T(8,128)}), f32[512,512]{0,1:T(8,128)}) %all-reduce.9.cloned.1.call-update) | async-done | bytes 1048592 | tf_op jit(solution)/shard_map/psum | solution.py:30
  783.7 2.7 copy.10
  786.4 1.4 fusion.1
  788.8 11.7 %cholesky.358 = f32[128,128]{1,0:T(8,128)S(1)} custom-call(f32[128,128]{1,0:T(8,128)S(1)} %cholesky.439), custom_call_target="Cholesky" | custom-call | tf_op jit(solution)/shard_map/jit(cholesky)/cholesky | solution.py:31
  800.7 9.8 custom-call.31
  813.1 11.7 %cholesky.377 = f32[128,128]{1,0:T(8,128)S(1)} custom-call(f32[128,128]{1,0:T(8,128)S(1)} %cholesky.443), custom_call_target="Cholesky" | custom-call | tf_op jit(solution)/shard_map/jit(cholesky)/cholesky | solution.py:31
  826.2 9.9 custom-call.32
  837.7 11.7 %cholesky.398 = f32[128,128]{1,0:T(8,128)S(1)} custom-call(f32[128,128]{1,0:T(8,128)S(1)} %cholesky.448), custom_call_target="Cholesky" | custom-call | tf_op jit(solution)/shard_map/jit(cholesky)/cholesky | solution.py:31
  850.1 9.8 custom-call.33
  861.3 11.7 %cholesky.415 = f32[128,128]{1,0:T(8,128)S(1)} custom-call(f32[128,128]{1,0:T(8,128)S(1)} %convolution_subtract_fusion.10), custom_call_target="Cholesky" | custom-call | tf_op jit(solution)/shard_map/jit(cholesky)/cholesky | solution.py:31
  877.7 11.7 %while.5 = (s32[]{:T(128)}, f32[512,512]{1,0:T(8,128)}, s32[4,2]{0,1:T(2,128)S(1)}, f32[4,128,128]{2,1,0:T(8,128)S(1)}, s32[]{:T(128)}) while((s32[]{:T(128)}, f32[512,512]{1,0:T(8,128)}, s32[4,2]{0,1:T(2,128)S(1)}, f32[4,128,128]{2,1,0:T(8,128)S(1)}, s32[]{:T(128)}) %tuple.72), condition=%wide.while_cond.clone, body=%wide.while_body.clone.sunk | while | flops 2 | bytes 131181 | solution.py:32
  878.4 2.3 bitcast_dynamic-update-slice_fusion.5
  881.4 2.3 bitcast_dynamic-update-slice_fusion.5
  884.3 2.3 bitcast_dynamic-update-slice_fusion.5
  887.2 2.2 bitcast_dynamic-update-slice_fusion.5
  889.4 39.3 %custom-call.34 = f32[4,128,128]{1,2,0:T(8,128)S(1)} custom-call(f32[4,128,128]{2,1,0:T(8,128)S(1)} %get-tuple-element.22), custom_call_target="InvertDiagBlocksLowerTriangular" | custom-call | tf_op jit(solution)/shard_map/jit(_solve_triangular)/triangular_solve | solution.py:32
  930.6 1.5 convolution_subtract_fusion.3
  932.5 1.8 convolution_subtract_fusion.2
  934.5 3.7 convolution_bitcast_fusion
  938.2 97.0 %reduce-scatter.2.cloned.1.call-done = f32[384,512]{0,1:T(8,128)} async-done(((f32[3072,512]{0,1:T(8,128)}), f32[384,512]{0,1:T(8,128)}) %reduce-scatter.2.cloned.1.call-update) | async-done | bytes 786448 | tf_op jit(solution)/shard_map/reduce_scatter | solution.py:34
  (100 shorter events, 37.1 us)
Async XLA Ops:
  6.5 167.9 %copy-start = (bf16[3072,256]{1,0:T(8,128)(2,1)S(1)}, bf16[3072,256]{1,0:T(8,128)(2,1)}, u32[]{:S(2)}) copy-start(bf16[3072,256]{1,0:T(8,128)(2,1)} %param.5) | copy-start | bytes 4718596
  6.5 167.9 %all-gather.4.cloned.1.call-start = ((), (), s32[]{:S(2)}) async-start(), calls=%async_computation.1 | async-start | bytes 14155776 | tf_op jit(solution)/shard_map/all_gather | solution.py:21
  7.3 255.2 %all-gather.6.cloned.1.call-start = ((), (), s32[]{:S(2)}) async-start(), calls=%async_computation.3 | async-start | bytes 4718592 | tf_op jit(solution)/shard_map/all_gather | solution.py:25
  8.0 363.1 %all-reduce.5.cloned.1.call-start = ((), (), s32[]{:S(2)}) async-start(), calls=%async_computation.2 | async-start | bytes 4194304 | tf_op jit(solution)/shard_map/psum | solution.py:22
  182.2 188.8 %copy-start.5 = (f32[256,512]{1,0:T(8,128)S(1)}, f32[256,512]{1,0:T(8,128)}, u32[]{:S(2)}) copy-start(f32[256,512]{1,0:T(8,128)} %param.6) | copy-start | bytes 1572868
  182.3 286.2 %all-reduce.7.cloned.1.call-start = ((), (), s32[]{:S(2)}) async-start(), calls=%async_computation.4 | async-start | bytes 2097152 | tf_op jit(solution)/shard_map/psum | solution.py:30
  379.4 310.0 %all-gather.8.cloned.1.call-start = ((), (), s32[]{:S(2)}) async-start(), calls=%async_computation.5 | async-start | bytes 4718592 | tf_op jit(solution)/shard_map/all_gather | solution.py:25
  468.5 2.7 copy-start.1
  472.6 1.0 copy-start.4
  619.7 164.0 %all-reduce.9.cloned.1.call-start = ((), (), s32[]{:S(2)}) async-start(), calls=%async_computation.6 | async-start | bytes 2097152 | tf_op jit(solution)/shard_map/psum | solution.py:30
  697.9 337.3 %reduce-scatter.2.cloned.1.call-start = ((), (), s32[]{:S(2)}) async-start(), calls=%async_computation.7 | async-start | bytes 7077888 | tf_op jit(solution)/shard_map/reduce_scatter | solution.py:34
  783.7 2.7 copy-start.2
  787.8 1.0 copy-start.3
Sparse Core Ops, SparseCore 0:
  9.5 164.8 all-gather.3
  176.7 70.8 all-gather.5
  250.1 120.8 all-reduce.4
  379.5 88.8 all-reduce.6
  619.8 69.5 all-gather.7
  698.0 85.6 all-reduce.8
  938.4 96.8 reduce-scatter.1
where the time goes:
time: 1050 us; the launch traced here: 1040 us
  waiting for transfers between devices  617 us (59%)
  other arithmetic  246 us (23%)
  blocking collectives  78.1 us (7%)
  matrix products  50.6 us (5%)
  local copies, waits for them, and re-layouts  32.1 us (3%)
  between operations  19.8 us (2%)
    psum x2, waiting for transfers between devices, on_device(): correlation = lax.psum(local_correlation, 'batch')  174 us
    all_gather x1, waiting for transfers between devices, on_device(): lax.all_gather(bases, 'batch', axis=1, tiled=True)  166 us
    another operation x29, other arithmetic, on_device(): factor = jnp.linalg.cholesky(correlation)  158 us
    psum x1, waiting for transfers between devices, on_device(): gram_rows = lax.psum(partial_value, 'rows')  109 us
    reduce_scatter x1, waiting for transfers between devices, on_device(): lax.psum_scatter(jnp.dot(bases, q_low, preferred_element_type=jnp.float32...  97 us
    another operation x5, other arithmetic, on_device(): q_own = jax.scipy.linalg.solve_triangular(factor, lifted.T, lower=True).T  81.3 us
    psum x1, blocking collectives, on_device(): lax.psum(jnp.sum(jnp.square(bases.astype(jnp.float32))), ('rows', 'batch'))  78.1 us
    all_gather x2, waiting for transfers between devices, on_device(): q_full = lax.all_gather(q_own, 'batch', axis=0, tiled=True)  69.7 us
  transfers between devices with their start and end apart: 7, of which 6 were waited for; matrix products, arithmetic and copies ran while one was open for 1% of the time, Pallas kernels for 0%

commit v1 on v0

--- a/solution.py
+++ b/solution.py
@@ -27,7 +27,8 @@
         local_correlation = lax.dot_general(
             lifted, lifted, (((0,), (0,)), ((), ())), precision=lax.Precision.HIGHEST
         )
-        correlation = lax.psum(local_correlation, "batch")
+        pieces = lax.all_gather(local_correlation, "batch")
+        correlation = jnp.sum(pieces, axis=0)
         factor = jnp.linalg.cholesky(correlation)
         q_own = jax.scipy.linalg.solve_triangular(factor, lifted.T, lower=True).T
     q_low = q_own.astype(jnp.bfloat16)

time: 1050 us -> 1100 us (1.048)
  waiting for transfers between devices: 617 us -> 658 us
    all_gather x0 -> x2, waiting for transfers between devices: none -> 215 us  [on_device(): pieces = lax.all_gather(local_correlation, 'batch')]
    psum x2 -> x0, waiting for transfers between devices: 174 us -> none  [on_device(): correlation = lax.psum(local_correlation, 'batch')]
where the time goes in v1:
time: 1100 us; the launch traced here: 1090 us
  waiting for transfers between devices  658 us (60%)
  other arithmetic  254 us (23%)
  blocking collectives  78.1 us (7%)
  matrix products  50.5 us (5%)
  local copies, waits for them, and re-layouts  29.2 us (3%)
  between operations  19.9 us (2%)
    all_gather x2, waiting for transfers between devices, on_device(): pieces = lax.all_gather(local_correlation, 'batch')  215 us
    all_gather x1, waiting for transfers between devices, on_device(): lax.all_gather(bases, 'batch', axis=1, tiled=True)  166 us
    another operation x29, other arithmetic, on_device(): factor = jnp.linalg.cholesky(correlation)  158 us
    psum x1, waiting for transfers between devices, on_device(): gram_rows = lax.psum(partial_value, 'rows')  109 us
    reduce_scatter x1, waiting for transfers between devices, on_device(): lax.psum_scatter(jnp.dot(bases, q_low, preferred_element_type=jnp.float32...  96.7 us
    another operation x5, other arithmetic, on_device(): q_own = jax.scipy.linalg.solve_triangular(factor, lifted.T, lower=True).T  80.9 us
    psum x1, blocking collectives, on_device(): lax.psum(jnp.sum(jnp.square(bases.astype(jnp.float32))), ('rows', 'batch'))  78.1 us
    all_gather x2, waiting for transfers between devices, on_device(): q_full = lax.all_gather(q_own, 'batch', axis=0, tiled=True)  69.5 us
  transfers between devices with their start and end apart: 7, of which 6 were waited for; matrix products, arithmetic and copies ran while one was open for 1% of the time, Pallas kernels for 0%

profile of v1, /device:TPU:0, one launch (start us, length us, event | category | flops | bytes accessed | tf_op | source)
XLA Modules:
  0.0 1091.0 jit_solution(9517130713374095499)
XLA Ops:
  8.1 166.4 %all-gather.8.cloned.1.call-done = bf16[3072,2048]{1,0:T(8,128)(2,1)} async-done(((bf16[3072,256]{1,0:T(8,128)(2,1)}), bf16[3072,2048]{1,0:T(8,128)(2,1)}) %all-gather.8.cloned.1.call-update) | async-done | bytes 12582928 | tf_op jit(solution)/shard_map/all_gather | solution.py:21
  174.4 7.8 fusion.76
  182.3 1.4 multiply_reduce_fusion
  183.7 78.1 %psum.15 = f32[]{:T(128)} all-reduce(f32[]{:T(128)} %multiply_reduce_fusion), channel_id=1, replica_groups=mesh['rows'=16,'batch'=8] {'rows','batch'}, use_global_device_ids=true, to_apply=%region_2.0 | all-reduce | flops 1 | bytes 8 | tf_op jit(solution)/shard_map/psum | solution.py:19
  262.5 108.8 %all-reduce.3.cloned.1.call-done = f32[256,2048]{1,0:T(8,128)} async-done(((f32[256,2048]{1,0:T(8,128)}), f32[256,2048]{1,0:T(8,128)}) %all-reduce.3.cloned.1.call-update) | async-done | bytes 2097168 | tf_op jit(solution)/shard_map/psum | solution.py:22
  371.2 6.2 fusion
  377.5 2.0 fusion.77
  380.1 109.1 %all-gather.14.cloned.1.call-done = f32[4096,512]{1,0:T(8,128)} async-done(((f32[512,512]{1,0:T(8,128)}), f32[4096,512]{1,0:T(8,128)}) %all-gather.14.cloned.1.call-update) | async-done | bytes 8388624 | tf_op jit(solution)/shard_map/all_gather | solution.py:30
  489.1 4.5 reduce_sum.28
  495.0 1.4 fusion.2
  497.4 11.7 %cholesky.286 = f32[128,128]{1,0:T(8,128)S(1)} custom-call(f32[128,128]{1,0:T(8,128)S(1)} %cholesky.426), custom_call_target="Cholesky" | custom-call | tf_op jit(solution)/shard_map/jit(cholesky)/cholesky | solution.py:32
  509.2 9.8 custom-call.27
  521.6 11.8 %cholesky.305 = f32[128,128]{1,0:T(8,128)S(1)} custom-call(f32[128,128]{1,0:T(8,128)S(1)} %cholesky.430), custom_call_target="Cholesky" | custom-call | tf_op jit(solution)/shard_map/jit(cholesky)/cholesky | solution.py:32
  533.4 9.8 custom-call.28
  544.8 11.7 %cholesky.326 = f32[128,128]{1,0:T(8,128)S(1)} custom-call(f32[128,128]{1,0:T(8,128)S(1)} %cholesky.435), custom_call_target="Cholesky" | custom-call | tf_op jit(solution)/shard_map/jit(cholesky)/cholesky | solution.py:32
  557.3 9.8 custom-call.29
  568.5 11.9 %cholesky.343 = f32[128,128]{1,0:T(8,128)S(1)} custom-call(f32[128,128]{1,0:T(8,128)S(1)} %convolution_subtract_fusion.11), custom_call_target="Cholesky" | custom-call | tf_op jit(solution)/shard_map/jit(cholesky)/cholesky | solution.py:32
  585.4 11.5 %while.4 = (s32[]{:T(128)}, f32[512,512]{1,0:T(8,128)}, s32[4,2]{0,1:T(2,128)S(1)}, f32[4,128,128]{2,1,0:T(8,128)S(1)}, s32[]{:T(128)}) while((s32[]{:T(128)}, f32[512,512]{1,0:T(8,128)}, s32[4,2]{0,1:T(2,128)S(1)}, f32[4,128,128]{2,1,0:T(8,128)S(1)}, s32[]{:T(128)}) %tuple.52), condition=%wide.while_cond, body=%wide.while_body.sunk | while | flops 2 | bytes 131181 | solution.py:33
  586.1 2.2 bitcast_dynamic-update-slice_fusion.4
  589.0 2.2 bitcast_dynamic-update-slice_fusion.4
  591.9 2.2 bitcast_dynamic-update-slice_fusion.4
  594.8 2.2 bitcast_dynamic-update-slice_fusion.4
  596.9 39.3 %custom-call.30 = f32[4,128,128]{1,2,0:T(8,128)S(1)} custom-call(f32[4,128,128]{2,1,0:T(8,128)S(1)} %get-tuple-element.21), custom_call_target="InvertDiagBlocksLowerTriangular" | custom-call | tf_op jit(solution)/shard_map/jit(_solve_triangular)/triangular_solve | solution.py:33
  638.1 1.5 convolution_subtract_fusion.6
  640.0 1.7 convolution_subtract_fusion.5
  643.2 69.4 %all-gather.12.cloned.1.call-done = f32[2048,512]{1,0:T(8,128)} async-done(((f32[256,512]{1,0:T(8,128)}), f32[2048,512]{1,0:T(8,128)}) %all-gather.12.cloned.1.call-update) | async-done | bytes 4194320 | tf_op jit(solution)/shard_map/all_gather | solution.py:25
  712.6 6.3 bitcast_add_fusion.2
  718.9 2.1 fusion.3
  721.5 105.9 %all-gather.16.cloned.1.call-done = f32[4096,512]{1,0:T(8,128)} async-done(((f32[512,512]{1,0:T(8,128)}), f32[4096,512]{1,0:T(8,128)}) %all-gather.16.cloned.1.call-update) | async-done | bytes 8388624 | tf_op jit(solution)/shard_map/all_gather | solution.py:30
  827.4 4.5 reduce_sum.29
  833.2 1.4 fusion.1
  835.7 11.7 %cholesky.358 = f32[128,128]{1,0:T(8,128)S(1)} custom-call(f32[128,128]{1,0:T(8,128)S(1)} %cholesky.439), custom_call_target="Cholesky" | custom-call | tf_op jit(solution)/shard_map/jit(cholesky)/cholesky | solution.py:32
  847.5 9.8 custom-call.31
  859.9 11.9 %cholesky.377 = f32[128,128]{1,0:T(8,128)S(1)} custom-call(f32[128,128]{1,0:T(8,128)S(1)} %cholesky.443), custom_call_target="Cholesky" | custom-call | tf_op jit(solution)/shard_map/jit(cholesky)/cholesky | solution.py:32
  873.1 9.8 custom-call.32
  884.5 11.7 %cholesky.398 = f32[128,128]{1,0:T(8,128)S(1)} custom-call(f32[128,128]{1,0:T(8,128)S(1)} %cholesky.448), custom_call_target="Cholesky" | custom-call | tf_op jit(solution)/shard_map/jit(cholesky)/cholesky | solution.py:32
  896.9 9.8 custom-call.33
  908.2 11.9 %cholesky.415 = f32[128,128]{1,0:T(8,128)S(1)} custom-call(f32[128,128]{1,0:T(8,128)S(1)} %convolution_subtract_fusion.10), custom_call_target="Cholesky" | custom-call | tf_op jit(solution)/shard_map/jit(cholesky)/cholesky | solution.py:32
  924.6 11.7 %while.5 = (s32[]{:T(128)}, f32[512,512]{1,0:T(8,128)}, s32[4,2]{0,1:T(2,128)S(1)}, f32[4,128,128]{2,1,0:T(8,128)S(1)}, s32[]{:T(128)}) while((s32[]{:T(128)}, f32[512,512]{1,0:T(8,128)}, s32[4,2]{0,1:T(2,128)S(1)}, f32[4,128,128]{2,1,0:T(8,128)S(1)}, s32[]{:T(128)}) %tuple.72), condition=%wide.while_cond.clone, body=%wide.while_body.clone.sunk | while | flops 2 | bytes 131181 | solution.py:33
  925.2 2.3 bitcast_dynamic-update-slice_fusion.5
  928.2 2.3 bitcast_dynamic-update-slice_fusion.5
  931.1 2.3 bitcast_dynamic-update-slice_fusion.5
  934.1 2.2 bitcast_dynamic-update-slice_fusion.5
  936.3 39.3 %custom-call.34 = f32[4,128,128]{1,2,0:T(8,128)S(1)} custom-call(f32[4,128,128]{2,1,0:T(8,128)S(1)} %get-tuple-element.22), custom_call_target="InvertDiagBlocksLowerTriangular" | custom-call | tf_op jit(solution)/shard_map/jit(_solve_triangular)/triangular_solve | solution.py:33
  977.5 1.5 convolution_subtract_fusion.3
  979.3 1.8 convolution_subtract_fusion.2
  981.4 3.7 convolution_bitcast_fusion
  985.1 96.7 %reduce-scatter.2.cloned.1.call-done = f32[384,512]{0,1:T(8,128)} async-done(((f32[3072,512]{0,1:T(8,128)}), f32[384,512]{0,1:T(8,128)}) %reduce-scatter.2.cloned.1.call-update) | async-done | bytes 786448 | tf_op jit(solution)/shard_map/reduce_scatter | solution.py:35
  (98 shorter events, 39.2 us)
Async XLA Ops:
  6.5 167.9 %copy-start = (bf16[3072,256]{1,0:T(8,128)(2,1)S(1)}, bf16[3072,256]{1,0:T(8,128)(2,1)}, u32[]{:S(2)}) copy-start(bf16[3072,256]{1,0:T(8,128)(2,1)} %param.5) | copy-start | bytes 4718596
  6.5 167.9 %all-gather.8.cloned.1.call-start = ((), (), s32[]{:S(2)}) async-start(), calls=%async_computation.1 | async-start | bytes 14155776 | tf_op jit(solution)/shard_map/all_gather | solution.py:21
  7.3 255.2 %all-gather.10.cloned.1.call-start = ((), (), s32[]{:S(2)}) async-start(), calls=%async_computation.3 | async-start | bytes 4718592 | tf_op jit(solution)/shard_map/all_gather | solution.py:25
  8.0 363.2 %all-reduce.3.cloned.1.call-start = ((), (), s32[]{:S(2)}) async-start(), calls=%async_computation.2 | async-start | bytes 4194304 | tf_op jit(solution)/shard_map/psum | solution.py:22
  182.2 189.0 %copy-start.3 = (f32[256,512]{1,0:T(8,128)S(1)}, f32[256,512]{1,0:T(8,128)}, u32[]{:S(2)}) copy-start(f32[256,512]{1,0:T(8,128)} %param.6) | copy-start | bytes 1572868
  182.3 306.9 %all-gather.14.cloned.1.call-start = ((), (), s32[]{:S(2)}) async-start(), calls=%async_computation.6 | async-start | bytes 9437184 | tf_op jit(solution)/shard_map/all_gather | solution.py:30
  379.5 333.1 %all-gather.12.cloned.1.call-start = ((), (), s32[]{:S(2)}) async-start(), calls=%async_computation.4 | async-start | bytes 4718592 | tf_op jit(solution)/shard_map/all_gather | solution.py:25
  496.4 1.0 copy-start.2
  643.1 184.3 %all-gather.16.cloned.1.call-start = ((), (), s32[]{:S(2)}) async-start(), calls=%async_computation.7 | async-start | bytes 9437184 | tf_op jit(solution)/shard_map/all_gather | solution.py:30
  721.1 360.7 %reduce-scatter.2.cloned.1.call-start = ((), (), s32[]{:S(2)}) async-start(), calls=%async_computation.5 | async-start | bytes 7077888 | tf_op jit(solution)/shard_map/reduce_scatter | solution.py:35
  834.7 1.0 copy-start.1
Sparse Core Ops, SparseCore 0:
  9.5 164.8 all-gather.7
  176.7 70.8 all-gather.9
  250.1 121.0 all-reduce.2
  379.7 109.4 all-gather.13
  643.2 69.3 all-gather.11
  721.2 106.1 all-gather.15
  985.2 96.5 reduce-scatter.1
